TPU v7x, 32 devices: a whole 2x2x4 slice. The times are simulated.
32 devices in a mesh: grp: 4 (over y, x), line: 8 (over z, core).
Axes of the slice: x: 2, y: 2, z: 4, core: 2. Of those that a mesh axis runs over, the one named last changes fastest.
Arguments:
- velocity: bfloat16 [3, 1536, 96, 512], P(None, 'line', 'grp'), may hold values from -6 to 6
- vorticity: bfloat16 [3, 1536, 96, 512], P(None, 'line', 'grp'), may hold values from -6 to 6
- wall_velocity: float32 [2, 256, 96, 1536], P(None, ('grp', 'line')), may hold values from -6 to 6
- wall_vorticity: float32 [2, 256, 96, 1536], P(None, ('grp', 'line')), may hold values from -6 to 6
- keep_mask: int32 [256, 96], P(('grp', 'line')), may hold values from 0 to 1, as said below
- derivative_band: float32 [7, 1536], replicated, may hold values from -3 to 3
- eigenvalues: float32 [1536], replicated, may hold values from 0.25 to 4
- eigenbasis: float32 [1536, 1536], replicated, may hold values from -0.15625 to 0.15625
Outputs:
- new_velocity: float32 [2, 256, 96, 1536], P(None, ('grp', 'line'))
- new_vorticity: float32 [2, 256, 96, 1536], P(None, ('grp', 'line'))
Inputs may be any that keep to these rules, and one draw needn't show every extreme that they name: keep_mask is 0 wherever kx >= 170, or 32 <= kz < 64.
All inputs are finite; a program needn't handle non-finite values.
Results may differ from a plain program's by a relative error of at most 0.0003.
Values sent between devices are 32-bit elements; how exact they have to be, the bound alone decides.
A program may use at most 384 MiB of HBM per device.

v0:
```python
import math
import jax
import jax.numpy as jnp
from jax import lax
from jax.sharding import PartitionSpec as P

HIGHEST_PRECISION = lax.Precision.HIGHEST


def phase_table(indices, points):
    index_cols = jnp.arange(points, dtype=jnp.int32)[None, :]
    phase_angle = (indices[:, None] * index_cols % points).astype(jnp.float32) * (
        2.0 * math.pi / points
    )
    norm_scale = 1.0 / math.sqrt(points)
    return (jnp.cos(phase_angle) * norm_scale, jnp.sin(phase_angle) * norm_scale)


def signed_wave(indices, points):
    signed_index = jnp.where(indices < points // 2, indices, indices - points)
    return signed_index.astype(jnp.float32) / (points / 2.0)


def curl_terms(spectra, stream_wave, span_wave):
    slope_source = jnp.stack(
        [
            -stream_wave * spectra[0, 1] - span_wave * spectra[2, 1],
            stream_wave * spectra[0, 0] + span_wave * spectra[2, 0],
        ]
    )
    normal_term = jnp.stack(
        [
            -span_wave * spectra[0, 1] + stream_wave * spectra[2, 1],
            span_wave * spectra[0, 0] - stream_wave * spectra[2, 0],
        ]
    )
    return (slope_source, normal_term)


def banded(padded, band_rows, extent):
    summed = band_rows[0] * padded[..., 0:extent]
    for offset in range(1, 7):
        summed = summed + band_rows[offset] * padded[..., offset : offset + extent]
    return summed


def local(
    velocity,
    vorticity,
    wall_velocity,
    wall_vorticity,
    keep_mask,
    derivative_band,
    eigenvalues,
    eigenbasis,
):
    group_count = lax.axis_size("grp")
    line_count = lax.axis_size("line")
    group_index = lax.axis_index("grp")
    line_index = lax.axis_index("line")
    moving = velocity.astype(jnp.float32)
    turning = vorticity.astype(jnp.float32)
    lamb_vector = jnp.stack(
        [
            moving[1] * turning[2] - moving[2] * turning[1],
            moving[2] * turning[0] - moving[0] * turning[2],
            moving[0] * turning[1] - moving[1] * turning[0],
        ]
    )
    slab_depth = lamb_vector.shape[1]
    span_share = lamb_vector.shape[2]
    stream_points = lamb_vector.shape[3]
    span_points = span_share * group_count
    stream_modes = stream_points // 2
    group_modes = stream_modes // group_count
    line_modes = group_modes // line_count
    span_keep = span_points // 3
    wall_points = wall_velocity.shape[3]
    span_list = jnp.concatenate(
        [
            jnp.arange(span_keep, dtype=jnp.int32),
            jnp.arange(span_points - span_keep, span_points, dtype=jnp.int32),
        ]
    )
    span_count = span_list.shape[0]
    stream_cosine, stream_sine = phase_table(
        jnp.arange(stream_modes, dtype=jnp.int32), stream_points
    )
    stream_table = jnp.stack(
        [
            stream_cosine.reshape(group_count, group_modes, stream_points),
            -stream_sine.reshape(group_count, group_modes, stream_points),
        ],
        1,
    )
    stream_table = stream_table.reshape(2 * stream_modes, stream_points)
    stream_spectra = jnp.einsum(
        "rx,cx->rc",
        lamb_vector.reshape(-1, stream_points),
        stream_table,
        precision=HIGHEST_PRECISION,
    )
    stream_spectra = stream_spectra.reshape(3, slab_depth, span_share, 2 * stream_modes)
    span_cosine, span_sine = phase_table(span_list, span_points)
    planes = lax.all_to_all(stream_spectra, "grp", split_axis=3, concat_axis=2, tiled=True)
    count_items = planes.shape[1]
    cosine_part = jnp.einsum("qz,fnzc->fcqn", span_cosine, planes, precision=HIGHEST_PRECISION)
    sine_part = jnp.einsum("qz,fnzc->fcqn", span_sine, planes, precision=HIGHEST_PRECISION)
    cosine_part = cosine_part.reshape(3, 2, group_modes, span_count, count_items)
    sine_part = sine_part.reshape(3, 2, group_modes, span_count, count_items)
    real_part = cosine_part[:, 0] + sine_part[:, 1]
    imag_part = cosine_part[:, 1] - sine_part[:, 0]
    local_modes = jnp.stack([real_part, imag_part], 1)
    span_wave = signed_wave(span_list, span_points)[:, None]
    device_modes = (group_index * line_count + line_index) * line_modes + jnp.arange(
        line_modes, dtype=jnp.int32
    )
    device_wave = (device_modes.astype(jnp.float32) / stream_modes)[:, None, None]
    whole_lines = lax.all_to_all(local_modes, "line", split_axis=2, concat_axis=4, tiled=True)
    wave_square = device_wave * device_wave + span_wave * span_wave
    slope_source, normal_term = curl_terms(whole_lines, device_wave, span_wave)
    padded = jnp.pad(slope_source, ((0, 0), (0, 0), (0, 0), (3, 3)))
    arrived = jnp.stack(
        [wave_square * whole_lines[1] - banded(padded, derivative_band, wall_points), normal_term]
    )
    middle = jnp.zeros((2, 2, line_modes, span_points - 2 * span_keep, wall_points), jnp.float32)
    arrived = jnp.concatenate(
        [arrived[:, :, :, :span_keep], middle, arrived[:, :, :, span_keep:]], 3
    )
    keep_weight = keep_mask.astype(jnp.float32)[:, :, None]
    right_side = jnp.stack([wall_velocity, wall_vorticity]) + keep_weight * arrived
    full_wave = signed_wave(jnp.arange(span_points, dtype=jnp.int32), span_points)[:, None]
    full_square = device_wave * device_wave + full_wave * full_wave
    eigen_coeffs = jnp.einsum(
        "fpkqy,yj->fpkqj", right_side, eigenbasis, precision=HIGHEST_PRECISION
    )
    eigen_coeffs = eigen_coeffs / (eigenvalues + full_square)
    solved = jnp.einsum("fpkqj,yj->fpkqy", eigen_coeffs, eigenbasis, precision=HIGHEST_PRECISION)
    return (solved[0], solved[1])


def solution(mesh):
    placed = (
        P(None, "line", "grp", None),
        P(None, "line", "grp", None),
        P(None, ("grp", "line"), None, None),
        P(None, ("grp", "line"), None, None),
        P(("grp", "line"), None),
        P(),
        P(),
        P(),
    )
    return jax.shard_map(
        local,
        mesh=mesh,
        in_specs=placed,
        out_specs=(P(None, ("grp", "line"), None, None), P(None, ("grp", "line"), None, None)),
        check_vma=False,
    )
```

profile of v0, /device:TPU:0, one launch (start us, length us, event | category | flops | bytes accessed | tf_op | source)
XLA Modules:
  0.0 1655.5 jit_solution(10274515562087793496)
XLA Ops:
  0.7 17.1 %convert_element_type.71 = f32[3,192,24,512]{3,2,1,0:T(8,128)} convert(bf16[3,192,24,512]{3,2,1,0:T(8,128)(2,1)} %param.8) | non-fusion elementwise | flops 7077888 | bytes 42467328 | tf_op jit(solution)/shard_map/convert_element_type | solution.py:61
  20.1 10.3 convert_element_type.72
  32.6 30.8 %multiply_subtract_fusion.2 = (f32[1,192,24,512]{3,2,1,0:T(8,128)}, f32[1,192,24,512]{3,2,1,0:T(8,128)}, f32[1,192,24,512]{3,2,1,0:T(8,128)}) fusion(f32[3,192,24,512]{3,2,1,0:T(8,128)} %convert_element_type.72, f32[3,192,24,512]{3,2,1,0:T(8,128)} %convert_element_type.71), kind=kLoop, calls=%fused_computation.37 | loop fusion | flops 21233664 | bytes 84934656 | tf_op jit(solution)/shard_map/sub | solution.py:65
  63.5 51.6 %fusion = f32[3,192,24,512]{3,2,1,0:T(8,128)} fusion(f32[512,512,1,1]{1,0,3,2:T(8,128)S(1)} %bitcast.85, f32[1,192,24,512]{3,2,1,0:T(8,128)} %get-tuple-element.14, f32[1,192,24,512]{3,2,1,0:T(8,128)} %get-tuple-element.13, f32[1,192,24,512]{3,2,1,0:T(8,128)} %get-tuple-element.12), kind=kOutput, calls=%fused_computation | convolution fusion | flops 43500699648 | bytes 57671680 | tf_op jit(solution)/shard_map/rx,cx->rc/dot_general | solution.py:97
  115.1 36.9 %copy.28 = f32[3,192,24,512]{1,2,0,3:T(8,128)} copy(f32[3,192,24,512]{3,2,1,0:T(8,128)} %fusion) | data formatting | bytes 56623104 | tf_op jit(solution)/shard_map/rx,cx->rc/dot_general | solution.py:97
  152.0 11.0 all-to-all-start
  163.1 408.4 %all-to-all-done = f32[3,192,24,512]{1,2,0,3:T(8,128)} async-done(((f32[3,192,24,512]{1,2,0,3:T(8,128)}), f32[3,192,24,512]{1,2,0,3:T(8,128)}, u32[]{:S(2)}, u32[]{:S(2)}) %all-to-all-start) | async-done | bytes 28311584 | tf_op jit(solution)/shard_map/all_to_all | solution.py:105
  571.6 34.4 %copy.29 = f32[3,192,24,4,128]{4,2,3,1,0:T(8,128)} copy(f32[3,192,24,4,128]{1,2,0,4,3:T(8,128)} %bitcast.5) | data formatting | bytes 56623104 | tf_op jit(solution)/shard_map/all_to_all | solution.py:105
  606.0 26.2 %convolution_bitcast_fusion.1 = f32[3,128,64,192]{1,2,3,0:T(8,128)} fusion(f32[3,192,96,128]{3,2,1,0:T(8,128)} %bitcast.80, s32[64]{0:T(128)S(1)} %get-tuple-element.11), kind=kOutput, calls=%fused_computation.40 | convolution fusion | flops 5435879424 | bytes 47186176 | tf_op jit(solution)/shard_map/qz,fnzc->fcqn/dot_general | solution.py:107
  632.3 26.2 %convolution_bitcast_fusion = f32[3,128,64,192]{1,2,3,0:T(8,128)} fusion(f32[3,192,96,128]{3,2,1,0:T(8,128)} %bitcast.81, s32[64]{0:T(128)S(1)} %get-tuple-element.11), kind=kOutput, calls=%fused_computation.39 | convolution fusion | flops 5435879424 | bytes 47186176 | tf_op jit(solution)/shard_map/qz,fnzc->fcqn/dot_general | solution.py:108
  658.4 25.1 %copy.30 = f32[3,128,64,192]{3,2,1,0:T(8,128)} copy(f32[3,128,64,192]{1,2,3,0:T(8,128)} %convolution_bitcast_fusion.1) | data formatting | bytes 37748736 | tf_op jit(solution)/shard_map/qz,fnzc->fcqn/transpose | solution.py:107
  683.5 25.1 %copy.31 = f32[3,128,64,192]{3,2,1,0:T(8,128)} copy(f32[3,128,64,192]{1,2,3,0:T(8,128)} %convolution_bitcast_fusion) | data formatting | bytes 37748736 | tf_op jit(solution)/shard_map/qz,fnzc->fcqn/transpose | solution.py:108
  708.6 27.5 %slice_add_fusion = (f32[3,1,64,64,192]{4,3,2,1,0:T(8,128)}, f32[3,1,64,64,192]{4,3,2,1,0:T(8,128)}) fusion(f32[3,2,64,64,192]{4,3,2,1,0:T(8,128)} %bitcast.83, f32[3,2,64,64,192]{4,3,2,1,0:T(8,128)} %bitcast.82), kind=kLoop, calls=%fused_computation.24 | loop fusion | flops 4718592 | bytes 56623104 | tf_op jit(solution)/shard_map/add | solution.py:111
  736.1 9.4 pad_maximum_fusion
  763.7 540.4 %all-to-all-done.1 = f32[3,2,64,64,192]{4,3,1,0,2:T(8,128)} async-done(((f32[3,2,64,64,192]{4,3,1,0,2:T(8,128)}), f32[3,2,64,64,192]{4,3,1,0,2:T(8,128)}, u32[]{:S(2)}, u32[]{:S(2)}) %all-to-all-start.1) | async-done | bytes 18874400 | tf_op jit(solution)/shard_map/all_to_all | solution.py:119
  1304.1 26.5 %copy.35 = f32[3,2,8,64,8,192]{5,4,3,2,1,0:T(8,128)} copy(f32[3,2,8,64,8,192]{5,3,1,0,2,4:T(8,128)} %bitcast.20) | data formatting | bytes 37748736 | tf_op jit(solution)/shard_map/all_to_all | solution.py:119
  1330.7 25.3 %all_to_all.33 = f32[3,2,8,64,1536]{4,3,2,1,0:T(8,128)} reshape(f32[3,2,8,64,8,192]{5,4,3,2,1,0:T(8,128)} %copy.35) | data formatting | bytes 37748736 | tf_op jit(solution)/shard_map/all_to_all | solution.py:119
  1355.9 17.5 %copy.33 = f32[3,2,64,64,192]{4,3,2,1,0:T(8,128)} copy(f32[3,2,64,64,192]{4,3,1,0,2:T(8,128)} %all-to-all-done.1) | data formatting | bytes 37748736 | tf_op jit(solution)/shard_map/all_to_all | solution.py:119
  1377.5 9.9 copy.34
  1387.4 9.5 squeeze.14
  1408.8 23.5 %subtract_bitcast_fusion = f32[1,2,8,64,1536]{4,3,2,1,0:T(8,128)} fusion(f32[2,8,64,1536]{3,2,1,0:T(8,128)} %pad_maximum_fusion.1, f32[2,8,64,1536]{3,2,1,0:T(8,128)} %squeeze.14, f32[1536]{0:T(1024)S(1)} %get-tuple-element.7, f32[1536]{0:T(1024)S(1)} %get-tuple-element.8, f32[1536]{0:T(1024)S(1)} %get-tuple-element.3, f32[1536]{0:T(1024)S(1)} %get-tuple-element.4, ...), kind=kLoop, calls=%fused_computation.44 | loop fusion | flops 23592960 | bytes 18919424 | tf_op jit(solution)/shard_map/stack | solution.py:123
  1438.6 105.2 %fusion.9 = f32[2,2,8,96,1536]{4,3,2,1,0:T(8,128)} fusion(f32[1,2,8,64,1536]{4,3,2,1,0:T(8,128)} %maximum_bitcast_fusion, f32[1,2,8,64,1536]{4,3,2,1,0:T(8,128)} %subtract_bitcast_fusion, f32[1,2,8,96,1536]{4,3,2,1,0:T(8,128)} %bitcast.86, f32[1,2,8,96,1536]{4,3,2,1,0:T(8,128)} %bitcast.87, f32[2,2,8,32,1536]{4,3,2,1,0:T(8,128)} %fusion.28, ...), kind=kOutput, calls=%fused_computation.11 | convolution fusion | flops 87015555072 | bytes 66063744 | tf_op jit(solution)/shard_map/fpkqy,yj->fpkqj/dot_general | solution.py:134
  1543.8 99.0 %fusion.19 = f32[2,2,8,96,1536]{4,3,2,1,0:T(8,128)} fusion(f32[2,2,8,96,1536]{4,3,2,1,0:T(8,128)} %fusion.9, f32[1536,1536]{1,0:T(8,128)} %param.15, f32[8,96,1536]{2,1,0:T(8,128)} %broadcast_add_fusion), kind=kOutput, calls=%fused_computation.21 | convolution fusion | flops 86977806336 | bytes 51904512 | tf_op jit(solution)/shard_map/fpkqj,yj->fpkqy/dot_general | solution.py:138
  1642.7 12.6 slice_bitcast_fusion
  (32 shorter events, 45.0 us)
Async XLA Ops:
  0.6 19.5 %copy-start = (bf16[3,192,24,512]{3,2,1,0:T(8,128)(2,1)S(1)}, bf16[3,192,24,512]{3,2,1,0:T(8,128)(2,1)}, u32[]{:S(2)}) copy-start(bf16[3,192,24,512]{3,2,1,0:T(8,128)(2,1)} %param.9) | copy-start | bytes 42467332
  152.0 419.6 %all-to-all-start = ((f32[3,192,24,512]{1,2,0,3:T(8,128)}), f32[3,192,24,512]{1,2,0,3:T(8,128)}, u32[]{:S(2)}, u32[]{:S(2)}) async-start(f32[3,192,24,512]{1,2,0,3:T(8,128)} %copy.28), calls=%async_computation | async-start | bytes 75497472 | tf_op jit(solution)/shard_map/all_to_all | solution.py:105
  754.2 6.6 copy-start.3
  754.2 6.7 copy-start.1
  754.2 7.0 copy-start.2
  754.2 550.0 %all-to-all-start.1 = ((f32[3,2,64,64,192]{4,3,1,0,2:T(8,128)}), f32[3,2,64,64,192]{4,3,1,0,2:T(8,128)}, u32[]{:S(2)}, u32[]{:S(2)}) async-start(f32[3,2,64,64,192]{4,3,1,0,2:T(8,128)} %copy.32), calls=%async_computation.1 | async-start | bytes 50331648 | tf_op jit(solution)/shard_map/all_to_all | solution.py:119
where the time goes:
time: 1660 us
  waiting for transfers between devices  949 us (57%)
  matrix products  308 us (19%)
  local copies, waits for them, and re-layouts  238 us (14%)
  other arithmetic  142 us (9%)
  starting transfers between devices  17.6 us (1%)
    all_to_all x1, waiting for transfers between devices, local(): lax.all_to_all(local_modes, 'line', split_axis=2, concat_axis=4, tiled=True)  540 us
    all_to_all x1, waiting for transfers between devices, local(): lax.all_to_all(stream_spectra, 'grp', split_axis=3, concat_axis=2, tiled=...  408 us
    dot_general x1, matrix products, local(): jnp.einsum('fpkqy,yj->fpkqj', right_side, eigenbasis, precision=HIGHEST_P...  105 us
    dot_general x1, matrix products, local(): jnp.einsum('fpkqj,yj->fpkqy', eigen_coeffs, eigenbasis, precision=HIGHEST...  99 us
    all_to_all x3, local copies, waits for them, and re-layouts, local(): lax.all_to_all(local_modes, 'line', split_axis=2, concat_axis=4, tiled=True)  69.3 us
    dot_general x1, matrix products, local(): jnp.einsum('rx,cx->rc', lamb_vector.reshape(-1, stream_points), stream_ta...  51.6 us
    dot_general x1, local copies, waits for them, and re-layouts, local(): jnp.einsum('rx,cx->rc', lamb_vector.reshape(-1, stream_points), stream_ta...  36.9 us
    all_to_all x1, local copies, waits for them, and re-layouts, local(): lax.all_to_all(stream_spectra, 'grp', split_axis=3, concat_axis=2, tiled=...  34.4 us
  transfers between devices with their start and end apart: 2, of which 2 were waited for; matrix products, arithmetic and copies ran while one was open for 0% of the time, Pallas kernels for 0%

commit v1 on v0

--- a/solution.py
+++ b/solution.py
@@ -102,7 +102,17 @@
     )
     stream_spectra = stream_spectra.reshape(3, slab_depth, span_share, 2 * stream_modes)
     span_cosine, span_sine = phase_table(span_list, span_points)
-    planes = lax.all_to_all(stream_spectra, "grp", split_axis=3, concat_axis=2, tiled=True)
+
+    def divide_scales_on_mesh(local_values, axis_key):
+        frame_out = lax.all_to_all(
+            jnp.stack(jnp.split(local_values, lax.axis_size(axis_key), 3), 0),
+            axis_name=axis_key,
+            split_axis=0,
+            concat_axis=0,
+        )
+        return jnp.concatenate(frame_out, axis=2)
+
+    planes = divide_scales_on_mesh(stream_spectra, "grp")
     count_items = planes.shape[1]
     cosine_part = jnp.einsum("qz,fnzc->fcqn", span_cosine, planes, precision=HIGHEST_PRECISION)
     sine_part = jnp.einsum("qz,fnzc->fcqn", span_sine, planes, precision=HIGHEST_PRECISION)

time: 1660 us -> 1550 us (0.934)
  waiting for transfers between devices: 949 us -> 848 us
  local copies, waits for them, and re-layouts: 238 us -> 208 us
  other arithmetic: 142 us -> 162 us
    all_to_all x1, waiting for transfers between devices: 408 us -> 307 us  [divide_scales_on_mesh(): lax.all_to_all(jnp.stack(jnp.split(local_values, lax.axis_size(axis_key),...]
    dot_general x1 -> x0, local copies, waits for them, and re-layouts: 36.9 us -> none  [local(): jnp.einsum('rx,cx->rc', lamb_vector.reshape(-1, stream_points), stream_ta...]
    all_to_all x1 -> x0, local copies, waits for them, and re-layouts: 34.4 us -> none  [local(): lax.all_to_all(stream_spectra, 'grp', split_axis=3, concat_axis=2, tiled=...]
    reshape x0 -> x1, local copies, waits for them, and re-layouts: none -> 21.4 us  [divide_scales_on_mesh(): return jnp.concatenate(frame_out, axis=2)]
    another operation x0 -> x1, other arithmetic: none -> 20.9 us  [divide_scales_on_mesh(): jnp.stack(jnp.split(local_values, lax.axis_size(axis_key), 3), 0)]
    another operation x0 -> x1, local copies, waits for them, and re-layouts: none -> 20.3 us  [divide_scales_on_mesh(): jnp.stack(jnp.split(local_values, lax.axis_size(axis_key), 3), 0)]
where the time goes in v1:
time: 1550 us; the launch traced here: 1540 us
  waiting for transfers between devices  848 us (55%)
  matrix products  308 us (20%)
  local copies, waits for them, and re-layouts  208 us (13%)
  other arithmetic  162 us (10%)
  starting transfers between devices  16 us (1%)
    all_to_all x1, waiting for transfers between devices, local(): lax.all_to_all(local_modes, 'line', split_axis=2, concat_axis=4, tiled=True)  540 us
    all_to_all x1, waiting for transfers between devices, divide_scales_on_mesh(): lax.all_to_all(jnp.stack(jnp.split(local_values, lax.axis_size(axis_key),...  307 us
    dot_general x1, matrix products, local(): jnp.einsum('fpkqy,yj->fpkqj', right_side, eigenbasis, precision=HIGHEST_P...  105 us
    dot_general x1, matrix products, local(): jnp.einsum('fpkqj,yj->fpkqy', eigen_coeffs, eigenbasis, precision=HIGHEST...  99 us
    all_to_all x3, local copies, waits for them, and re-layouts, local(): lax.all_to_all(local_modes, 'line', split_axis=2, concat_axis=4, tiled=True)  69.3 us
    dot_general x1, matrix products, local(): jnp.einsum('rx,cx->rc', lamb_vector.reshape(-1, stream_points), stream_ta...  51.6 us
    another operation x3, other arithmetic, local(): jnp.stack([wave_square * whole_lines[1] - banded(padded, derivative_band,...  31.9 us
  transfers between devices with their start and end apart: 2, of which 2 were waited for; matrix products, arithmetic and copies ran while one was open for 0% of the time, Pallas kernels for 0%

profile of v1, /device:TPU:0, one launch (start us, length us, event | category | flops | bytes accessed | tf_op | source)
XLA Modules:
  0.0 1543.0 jit_solution(3884449060299841971)
XLA Ops:
  0.7 17.1 %convert_element_type.71 = f32[3,192,24,512]{3,2,1,0:T(8,128)} convert(bf16[3,192,24,512]{3,2,1,0:T(8,128)(2,1)} %param.8) | non-fusion elementwise | flops 7077888 | bytes 42467328 | tf_op jit(solution)/shard_map/convert_element_type | solution.py:61
  20.1 10.3 convert_element_type.72
  32.6 30.8 %multiply_subtract_fusion.2 = (f32[1,192,24,512]{3,2,1,0:T(8,128)}, f32[1,192,24,512]{3,2,1,0:T(8,128)}, f32[1,192,24,512]{3,2,1,0:T(8,128)}) fusion(f32[3,192,24,512]{3,2,1,0:T(8,128)} %convert_element_type.72, f32[3,192,24,512]{3,2,1,0:T(8,128)} %convert_element_type.71), kind=kLoop, calls=%fused_computation.38 | loop fusion | flops 21233664 | bytes 84934656 | tf_op jit(solution)/shard_map/sub | solution.py:65
  63.5 51.6 %fusion = f32[3,192,24,512]{3,2,1,0:T(8,128)} fusion(f32[512,512,1,1]{1,0,3,2:T(8,128)S(1)} %bitcast.91, f32[1,192,24,512]{3,2,1,0:T(8,128)} %get-tuple-element.14, f32[1,192,24,512]{3,2,1,0:T(8,128)} %get-tuple-element.13, f32[1,192,24,512]{3,2,1,0:T(8,128)} %get-tuple-element.12), kind=kOutput, calls=%fused_computation | convolution fusion | flops 43500699648 | bytes 57671680 | tf_op jit(solution)/shard_map/rx,cx->rc/dot_general | solution.py:97
  115.1 20.3 %slice_bitcast_fusion.5 = (f32[1,3,192,24,128]{4,3,2,1,0:T(8,128)}, f32[1,3,192,24,128]{4,3,2,1,0:T(8,128)}, f32[1,3,192,24,128]{4,3,2,1,0:T(8,128)}, f32[1,3,192,24,128]{4,3,2,1,0:T(8,128)}) fusion(f32[3,192,24,512]{3,2,1,0:T(8,128)} %fusion), kind=kLoop, calls=%fused_computation.45 | loop fusion | bytes 56623104 | tf_op jit(solution)/shard_map/stack | solution.py:108
  135.5 20.9 %pad_maximum_fusion = f32[4,3,192,24,128]{4,3,2,1,0:T(8,128)} fusion(f32[1,3,192,24,128]{4,3,2,1,0:T(8,128)} %get-tuple-element.18, f32[1,3,192,24,128]{4,3,2,1,0:T(8,128)} %get-tuple-element.19, f32[1,3,192,24,128]{4,3,2,1,0:T(8,128)} %get-tuple-element.20, f32[1,3,192,24,128]{4,3,2,1,0:T(8,128)} %get-tuple-element.17), kind=kLoop, calls=%fused_computation.6 | loop fusion | flops 21233664 | bytes 56623104 | tf_op jit(solution)/shard_map/stack | solution.py:108
  165.9 307.2 %all-to-all-done = f32[4,3,192,24,128]{4,3,2,1,0:T(8,128)} async-done(((f32[4,3,192,24,128]{4,3,2,1,0:T(8,128)}), f32[4,3,192,24,128]{4,3,2,1,0:T(8,128)}, u32[]{:S(2)}, u32[]{:S(2)}) %all-to-all-start) | async-done | bytes 28311584 | tf_op jit(solution)/shard_map/all_to_all | solution.py:107
  473.1 21.4 %copy.19 = f32[3,192,4,24,128]{4,3,2,1,0:T(8,128)} copy(f32[3,192,4,24,128]{4,3,1,0,2:T(8,128)} %bitcast.9) | data formatting | bytes 56623104 | tf_op jit(solution)/shard_map/reshape | solution.py:113
  494.5 26.2 %convolution_bitcast_fusion.1 = f32[3,128,64,192]{1,2,3,0:T(8,128)} fusion(f32[3,192,96,128]{3,2,1,0:T(8,128)} %bitcast.86, s32[64]{0:T(128)S(1)} %get-tuple-element.11), kind=kOutput, calls=%fused_computation.41 | convolution fusion | flops 5435879424 | bytes 47186176 | tf_op jit(solution)/shard_map/qz,fnzc->fcqn/dot_general | solution.py:117
  520.7 26.1 %convolution_bitcast_fusion = f32[3,128,64,192]{1,2,3,0:T(8,128)} fusion(f32[3,192,96,128]{3,2,1,0:T(8,128)} %bitcast.87, s32[64]{0:T(128)S(1)} %get-tuple-element.11), kind=kOutput, calls=%fused_computation.40 | convolution fusion | flops 5435879424 | bytes 47186176 | tf_op jit(solution)/shard_map/qz,fnzc->fcqn/dot_general | solution.py:118
  546.9 25.1 %copy.20 = f32[3,128,64,192]{3,2,1,0:T(8,128)} copy(f32[3,128,64,192]{1,2,3,0:T(8,128)} %convolution_bitcast_fusion.1) | data formatting | bytes 37748736 | tf_op jit(solution)/shard_map/qz,fnzc->fcqn/transpose | solution.py:117
  572.0 25.1 %copy.21 = f32[3,128,64,192]{3,2,1,0:T(8,128)} copy(f32[3,128,64,192]{1,2,3,0:T(8,128)} %convolution_bitcast_fusion) | data formatting | bytes 37748736 | tf_op jit(solution)/shard_map/qz,fnzc->fcqn/transpose | solution.py:118
  597.1 27.5 %slice_add_fusion = (f32[3,1,64,64,192]{4,3,2,1,0:T(8,128)}, f32[3,1,64,64,192]{4,3,2,1,0:T(8,128)}) fusion(f32[3,2,64,64,192]{4,3,2,1,0:T(8,128)} %bitcast.89, f32[3,2,64,64,192]{4,3,2,1,0:T(8,128)} %bitcast.88), kind=kLoop, calls=%fused_computation.25 | loop fusion | flops 4718592 | bytes 56623104 | tf_op jit(solution)/shard_map/add | solution.py:121
  624.5 9.4 pad_maximum_fusion.1
  652.2 540.4 %all-to-all-done.1 = f32[3,2,64,64,192]{4,3,1,0,2:T(8,128)} async-done(((f32[3,2,64,64,192]{4,3,1,0,2:T(8,128)}), f32[3,2,64,64,192]{4,3,1,0,2:T(8,128)}, u32[]{:S(2)}, u32[]{:S(2)}) %all-to-all-start.1) | async-done | bytes 18874400 | tf_op jit(solution)/shard_map/all_to_all | solution.py:129
  1192.6 26.5 %copy.25 = f32[3,2,8,64,8,192]{5,4,3,2,1,0:T(8,128)} copy(f32[3,2,8,64,8,192]{5,3,1,0,2,4:T(8,128)} %bitcast.22) | data formatting | bytes 37748736 | tf_op jit(solution)/shard_map/all_to_all | solution.py:129
  1219.1 25.3 %all_to_all.20 = f32[3,2,8,64,1536]{4,3,2,1,0:T(8,128)} reshape(f32[3,2,8,64,8,192]{5,4,3,2,1,0:T(8,128)} %copy.25) | data formatting | bytes 37748736 | tf_op jit(solution)/shard_map/all_to_all | solution.py:129
  1244.4 17.5 %copy.23 = f32[3,2,64,64,192]{4,3,2,1,0:T(8,128)} copy(f32[3,2,64,64,192]{4,3,1,0,2:T(8,128)} %all-to-all-done.1) | data formatting | bytes 37748736 | tf_op jit(solution)/shard_map/all_to_all | solution.py:129
  1265.9 9.9 copy.24
  1275.8 9.5 squeeze.14
  1297.2 22.5 %subtract_bitcast_fusion = f32[1,2,8,64,1536]{4,3,2,1,0:T(8,128)} fusion(f32[2,8,64,1536]{3,2,1,0:T(8,128)} %pad_maximum_fusion.2, f32[2,8,64,1536]{3,2,1,0:T(8,128)} %squeeze.14, f32[1536]{0:T(1024)S(1)} %get-tuple-element.7, f32[1536]{0:T(1024)S(1)} %get-tuple-element.8, f32[1536]{0:T(1024)S(1)} %get-tuple-element.3, f32[1536]{0:T(1024)S(1)} %get-tuple-element.4, ...), kind=kLoop, calls=%fused_computation.49 | loop fusion | flops 23592960 | bytes 18919424 | tf_op jit(solution)/shard_map/stack | solution.py:133
  1326.0 105.2 %fusion.9 = f32[2,2,8,96,1536]{4,3,2,1,0:T(8,128)} fusion(f32[1,2,8,64,1536]{4,3,2,1,0:T(8,128)} %maximum_bitcast_fusion, f32[1,2,8,64,1536]{4,3,2,1,0:T(8,128)} %subtract_bitcast_fusion, f32[1,2,8,96,1536]{4,3,2,1,0:T(8,128)} %bitcast.92, f32[1,2,8,96,1536]{4,3,2,1,0:T(8,128)} %bitcast.93, f32[2,2,8,32,1536]{4,3,2,1,0:T(8,128)} %fusion.28, ...), kind=kOutput, calls=%fused_computation.12 | convolution fusion | flops 87015555072 | bytes 66063744 | tf_op jit(solution)/shard_map/fpkqy,yj->fpkqj/dot_general | solution.py:144
  1431.2 99.0 %fusion.19 = f32[2,2,8,96,1536]{4,3,2,1,0:T(8,128)} fusion(f32[2,2,8,96,1536]{4,3,2,1,0:T(8,128)} %fusion.9, f32[1536,1536]{1,0:T(8,128)} %param.15, f32[8,96,1536]{2,1,0:T(8,128)} %broadcast_add_fusion), kind=kOutput, calls=%fused_computation.22 | convolution fusion | flops 86977806336 | bytes 51904512 | tf_op jit(solution)/shard_map/fpkqj,yj->fpkqy/dot_general | solution.py:148
  1530.2 12.6 slice_bitcast_fusion
  (33 shorter events, 54.4 us)
Async XLA Ops:
  0.6 19.5 %copy-start = (bf16[3,192,24,512]{3,2,1,0:T(8,128)(2,1)S(1)}, bf16[3,192,24,512]{3,2,1,0:T(8,128)(2,1)}, u32[]{:S(2)}) copy-start(bf16[3,192,24,512]{3,2,1,0:T(8,128)(2,1)} %param.9) | copy-start | bytes 42467332
  156.3 316.8 %all-to-all-start = ((f32[4,3,192,24,128]{4,3,2,1,0:T(8,128)}), f32[4,3,192,24,128]{4,3,2,1,0:T(8,128)}, u32[]{:S(2)}, u32[]{:S(2)}) async-start(f32[4,3,192,24,128]{4,3,2,1,0:T(8,128)} %pad_maximum_fusion), calls=%async_computation | async-start | bytes 56623104 | tf_op jit(solution)/shard_map/all_to_all | solution.py:107
  642.6 6.6 copy-start.3
  642.6 6.7 copy-start.1
  642.6 7.0 copy-start.2
  642.6 550.0 %all-to-all-start.1 = ((f32[3,2,64,64,192]{4,3,1,0,2:T(8,128)}), f32[3,2,64,64,192]{4,3,1,0,2:T(8,128)}, u32[]{:S(2)}, u32[]{:S(2)}) async-start(f32[3,2,64,64,192]{4,3,1,0,2:T(8,128)} %copy.22), calls=%async_computation.1 | async-start | bytes 50331648 | tf_op jit(solution)/shard_map/all_to_all | solution.py:129
